TPU v7x, 32 devices: a whole 2x2x4 slice. The times are simulated.
32 devices in a mesh: gx: 2 (over y), gy: 4 (over z), gz: 4 (over x, core).
Axes of the slice: x: 2, y: 2, z: 4, core: 2. Of those that a mesh axis runs over, the one named last changes fastest.
Arguments:
- source_term: float32 [32, 8, 32, 512], P(None, 'gx', 'gy', 'gz'), may hold values from -16 to 16
- labels: int32 [8, 32, 512], P('gx', 'gy', 'gz'), may hold values from 0 to 5
- conductivity_table: float32 [6], replicated, may hold values from 0.05 to 1
- send_map: int32 [2, 4, 4, 256], P('gx', 'gy', 'gz'), may hold values from -1 to 4095, as said below
- owner_slots: int32 [4096], P(('gx', 'gy', 'gz')), may hold values from 0 to 255, as said below
- sensor_data: float32 [32, 128], replicated, may hold values from -6 to 6
Outputs:
- projections: float32 [3, 128, 4096], P(None, None, ('gx', 'gy', 'gz'))
- gram_blocks: float32 [6, 4096], P(None, ('gx', 'gy', 'gz'))
Inputs may be any that keep to these rules, and one draw needn't show every extreme that they name: `send_map`: entries q * 32 to q * 32 + 31 of row (sx, sy, iz) hold, in their first slots, the brick-local voxels (i * 8 + j) * 128 + k of the positions that this brick sends to owner q = ix * 4 + iy of the same iz, and -1 in the others; no voxel appears twice in a row; some brick fills all 32 slots of some owner. `owner_slots`: the 128 entries of owner d = (ix * 4 + iy) * 4 + iz name, each once, exactly the slots src * 32 + slot that the bricks src = sx * 4 + sy with the same iz fill for it.
All inputs are finite; a program needn't handle non-finite values.
Results may differ from a plain program's by a relative error of at most 0.00012.
Values sent between devices are 32-bit elements; how exact they have to be, the bound alone decides.
No kernel may reach another device: no remote copies, remote signals or barrier semaphores. Data moves between devices by JAX's collectives and lax.ppermute only.
A program may use at most 64 MiB of HBM per device.

v0:
```python
import jax
import jax.numpy as jnp
from jax import lax
from jax.sharding import PartitionSpec as P

mass_term = 0.25


def extended(block, sides, width):
    for axis, dim in sides:
        count = lax.axis_size(axis)
        forward = [(i, i + 1) for i in range(count - 1)]
        backward = [(target, source) for source, target in forward]
        low = lax.ppermute(
            lax.slice_in_dim(block, block.shape[dim] - width, None, axis=dim), axis, forward
        )
        high = lax.ppermute(lax.slice_in_dim(block, 0, width, axis=dim), axis, backward)
        block = jnp.concatenate([low, block, high], axis=dim)
    return block


def tissue(shifted, table):
    conductivity = jnp.zeros(shifted.shape, table.dtype)
    for tissue_level in range(table.shape[0]):
        conductivity = conductivity + jnp.where(
            shifted == tissue_level + 1, table[tissue_level], 0.0
        )
    inside = (shifted > 0).astype(table.dtype)
    return (conductivity, inside)


def neighbour_slices(dim_index, offset):
    selection = [slice(1, -1), slice(1, -1), slice(1, -1)]
    selection[dim_index] = slice(2, None) if offset > 0 else slice(0, -2)
    return tuple(selection)


def stencil(padded, conductivity, inside):
    leading = (slice(None),) * (padded.ndim - 3)
    middle = (slice(1, -1), slice(1, -1), slice(1, -1))
    centre = padded[leading + middle]
    own_cond = conductivity[middle]
    own_in = inside[middle]
    accumulated = mass_term * centre
    for dim_index in range(3):
        for offset in (-1, 1):
            beside_all = neighbour_slices(dim_index, offset)
            weight = 0.5 * (own_cond + conductivity[beside_all]) * own_in * inside[beside_all]
            accumulated = accumulated + weight * (centre - padded[leading + beside_all])
    return accumulated


def gram_rows(leadfield):
    entry_pairs = ((0, 0), (1, 1), (2, 2), (0, 1), (0, 2), (1, 2))
    return jnp.stack(
        [jnp.sum(leadfield[first] * leadfield[second], axis=0) for first, second in entry_pairs]
    )


def local_inner(first, second):
    return jnp.sum(first * second, axis=(1, 2, 3))


def per_sensor(values):
    return values[:, None, None, None]


def per_device(source_term, labels, conductivity_table, send_map, owner_slots, sensor_data):
    sensors, size_x, size_y, size_z = source_term.shape
    shifted = labels + 1
    label_pad = extended(shifted, (("gx", 0), ("gy", 1), ("gz", 2)), 2)
    conductivity, inside = tissue(label_pad, conductivity_table)
    source_pad = extended(source_term, (("gx", 1), ("gy", 2), ("gz", 3)), 2)
    applied = stencil(source_pad, conductivity, inside)
    inner_cond = conductivity[1:-1, 1:-1, 1:-1]
    inner_in = inside[1:-1, 1:-1, 1:-1]
    twice_applied = stencil(applied, inner_cond, inner_in)
    applied_core = applied[:, 1:-1, 1:-1, 1:-1]
    moment_zero, moment_one, moment_two, moment_three = lax.psum(
        (
            local_inner(source_term, source_term),
            local_inner(source_term, applied_core),
            local_inner(applied_core, applied_core),
            local_inner(applied_core, twice_applied),
        ),
        ("gx", "gy", "gz"),
    )
    first_step = moment_zero / moment_one
    residue = first_step * first_step * moment_two - moment_zero
    growth = 1.0 + residue / moment_zero
    curvature = (
        growth * growth * moment_one
        - 2.0 * growth * first_step * moment_two
        + first_step * first_step * moment_three
    )
    second_step = residue / curvature
    source_coef = first_step + second_step * growth
    applied_coef = second_step * first_step
    solution_pad = (
        per_sensor(source_coef) * source_pad[:, 1:-1, 1:-1, 1:-1]
        - per_sensor(applied_coef) * applied
    )
    cond_inner = conductivity[2:-2, 2:-2, 2:-2]
    voxel_local = jnp.maximum(send_map.reshape(-1), 0)
    index_x = voxel_local // (size_y * size_z)
    index_y = voxel_local // size_z % size_y
    index_z = voxel_local % size_z
    stride_y = size_z + 2
    stride_x = (size_y + 2) * (size_z + 2)
    centre = (index_x + 1) * stride_x + (index_y + 1) * stride_y + (index_z + 1)
    flattened = solution_pad.reshape(sensors, -1)
    cond_here = jnp.take(cond_inner.reshape(-1), voxel_local)

    def gradient(stride):
        upper = jnp.take(flattened, centre + stride, axis=1)
        lower = jnp.take(flattened, centre - stride, axis=1)
        return cond_here * ((upper - lower) * 0.5)

    columns = jnp.stack([gradient(stride_x), gradient(stride_y), gradient(1)])
    received = lax.all_to_all(columns, ("gx", "gy"), split_axis=2, concat_axis=2, tiled=True)
    owned = jnp.take(received, owner_slots, axis=2)
    projections = jnp.einsum("csp,st->ctp", owned, sensor_data, precision=lax.Precision.HIGHEST)
    return (projections, gram_rows(owned))


def solution(mesh):
    in_specs = (
        P(None, "gx", "gy", "gz"),
        P("gx", "gy", "gz"),
        P(),
        P("gx", "gy", "gz", None),
        P(("gx", "gy", "gz")),
        P(),
    )
    out_specs = (P(None, None, ("gx", "gy", "gz")), P(None, ("gx", "gy", "gz")))
    return jax.shard_map(
        per_device, mesh=mesh, in_specs=in_specs, out_specs=out_specs, check_vma=False
    )
```

profile of v0, /device:TPU:0, one launch (start us, length us, event | category | flops | bytes accessed | tf_op | source)
XLA Modules:
  0.0 188.7 jit_solution(1903327529436321746)
XLA Ops:
  1.4 4.9 %collective-permute-start.6 = (s32[2,8,128]{2,1,0:T(8,128)S(1)}, s32[2,8,128]{2,1,0:T(8,128)S(1)}, u32[]{:S(2)}, u32[]{:S(2)}) collective-permute-start(s32[2,8,128]{2,1,0:T(8,128)S(1)} %get-tuple-element.58), channel_id=1, source_target_pairs={{0,16},{1,17},{2,18},{3,19},{4,20},{5,21},{6,22},{7,23},{8,24},{9,... | collective-permute-start | bytes 24584 | tf_op jit(solution)/shard_map/ppermute | solution.py:14
  8.7 4.6 %collective-permute-start = (f32[32,2,8,128]{3,2,1,0:T(8,128)S(1)}, f32[32,2,8,128]{3,2,1,0:T(8,128)S(1)}, u32[]{:S(2)}, u32[]{:S(2)}) collective-permute-start(f32[32,2,8,128]{3,2,1,0:T(8,128)S(1)} %get-tuple-element.39), channel_id=1, source_target_pairs={{0,16},{1,17},{2,18},{3,19},{4,20},{5,21},{6,22},{7,23},{8,24},{9,... | collective-permute-start | bytes 786440 | tf_op jit(solution)/shard_map/ppermute | solution.py:14
  23.0 3.5 %collective-permute-start.8 = (s32[8,2,128]{2,1,0:T(2,128)S(1)}, s32[8,2,128]{2,1,0:T(2,128)S(1)}, u32[]{:S(2)}, u32[]{:S(2)}) collective-permute-start(s32[8,2,128]{2,1,0:T(2,128)S(1)} %get-tuple-element.56), channel_id=1, source_target_pairs={{0,4},{4,8},{8,12},{1,5},{5,9},{9,13},{2,6},{6,10},{10,14},{3,7},{... | collective-permute-start | bytes 24584 | tf_op jit(solution)/shard_map/ppermute | solution.py:14
  28.3 3.6 %collective-permute-done.9 = s32[8,2,128]{2,1,0:T(2,128)S(1)} collective-permute-done((s32[8,2,128]{2,1,0:T(2,128)S(1)}, s32[8,2,128]{2,1,0:T(2,128)S(1)}, u32[]{:S(2)}, u32[]{:S(2)}) %collective-permute-start.9) | collective-permute-done | bytes 8224 | tf_op jit(solution)/shard_map/ppermute | solution.py:17
  38.4 3.8 %select_add_fusion = f32[8,12,132]{2,1,0:T(8,128)S(1)} fusion(f32[]{:T(128)} %bitcast.8, f32[]{:T(128)} %bitcast.7, f32[]{:T(128)} %bitcast.6, f32[]{:T(128)} %bitcast.5, f32[]{:T(128)} %bitcast.4, f32[]{:T(128)} %bitcast.3, s32[8,12,2]{2,1,0:T(8,128)S(1)} %collective-permute-done.11, s32[8,2,128]{2,1,0:T(2,128)S(1)} %collective-permute-done.9, ...), kind=kLoop, calls=%fused_computation.79 | loop fusion | flops 291456 | bytes 101400 | tf_op jit(solution)/shard_map/add | solution.py:25
  43.7 3.5 %collective-permute-start.2 = (f32[32,8,2,128]{3,1,2,0:T(8,128)S(1)}, f32[32,8,2,128]{3,1,2,0:T(8,128)S(1)}, u32[]{:S(2)}, u32[]{:S(2)}) collective-permute-start(f32[32,8,2,128]{3,1,2,0:T(8,128)S(1)} %get-tuple-element.37), channel_id=1, source_target_pairs={{0,4},{4,8},{8,12},{1,5},{5,9},{9,13},{2,6},{6,10},{10,14},{3,7},{... | collective-permute-start | bytes 786440 | tf_op jit(solution)/shard_map/ppermute | solution.py:14
  51.9 4.7 %collective-permute-done.3 = f32[32,8,2,128]{3,1,2,0:T(8,128)S(1)} collective-permute-done((f32[32,8,2,128]{3,1,2,0:T(8,128)S(1)}, f32[32,8,2,128]{3,1,2,0:T(8,128)S(1)}, u32[]{:S(2)}, u32[]{:S(2)}) %collective-permute-start.3) | collective-permute-done | bytes 262176 | tf_op jit(solution)/shard_map/ppermute | solution.py:17
  63.8 4.2 %collective-permute-start.4 = (f32[32,8,12,2]{0,1,3,2:T(8,128)S(1)}, f32[32,8,12,2]{0,1,3,2:T(8,128)S(1)}, u32[]{:S(2)}, u32[]{:S(2)}) collective-permute-start(f32[32,8,12,2]{0,1,3,2:T(8,128)S(1)} %copy.93), channel_id=1, source_target_pairs={{0,1},{1,2},{2,3},{4,5},{5,6},{6,7},{8,9},{9,10},{10,11},{12,13},{... | collective-permute-start | bytes 73736 | tf_op jit(solution)/shard_map/ppermute | solution.py:14
  74.5 2.4 %copy.95 = f32[32,8,12,2]{3,1,2,0:T(8,128)} copy(f32[32,8,12,2]{0,1,3,2:T(8,128)S(1)} %collective-permute-done.4) | data formatting | bytes 49152 | tf_op jit(solution)/shard_map/ppermute | solution.py:14
  76.8 2.4 %copy.96 = f32[32,8,12,2]{3,1,2,0:T(8,128)} copy(f32[32,8,12,2]{0,1,3,2:T(8,128)S(1)} %collective-permute-done.5) | data formatting | bytes 49152 | tf_op jit(solution)/shard_map/ppermute | solution.py:17
  79.3 4.8 %pad_maximum_fusion = f32[32,8,12,132]{3,1,2,0:T(8,128)S(1)} fusion(f32[32,8,12,2]{3,1,2,0:T(8,128)} %copy.96, f32[32,8,2,128]{3,1,2,0:T(8,128)} %copy-done.11, f32[32,2,8,128]{3,1,2,0:T(2,128)} %copy-done.7, f32[32,4,8,128]{3,1,2,0:T(4,128)} %copy-done.4, f32[32,2,8,128]{3,1,2,0:T(2,128)S(1)} %copy.90, f32[32,8,2,128]{3,1,2,0:T(8,128)} %copy-done.9, ...), kind=kLoop, calls=%fused_computation.8 | loop fusion | flops 2433024 | bytes 3244032 | tf_op jit(solution)/shard_map/concatenate | solution.py:18
  84.3 7.2 %fusion.2 = f32[32,6,10,130]{3,1,2,0:T(8,128)S(1)} fusion(f32[32,8,12,2]{3,1,2,0:T(8,128)S(1)} %copy-done.3, f32[32,8,2,128]{3,1,2,0:T(8,128)S(1)} %copy-done.12, f32[32,8,2,128]{3,1,2,0:T(8,128)S(1)} %copy-done.10, f32[32,2,8,128]{3,1,2,0:T(2,128)S(1)} %copy-done.8, f32[32,4,8,128]{3,1,2,0:T(4,128)S(1)} %copy-done.5, f32[32,2,8,128]{3,1,2,0:T(2,128)S(1)} %copy.90, ...), kind=kLoop, calls=%fused_computation.12 | loop fusion | flops 7238400 | bytes 7799616 | tf_op jit(solution)/shard_map/add | solution.py:49
  95.4 41.9 %all-reduce = (f32[32]{0:T(128)S(1)}, f32[32]{0:T(128)S(1)}, f32[32]{0:T(128)S(1)}, f32[32]{0:T(128)S(1)}) all-reduce(f32[32]{0:T(128)S(1)} %get-tuple-element.15, f32[32]{0:T(128)S(1)} %get-tuple-element.14, f32[32]{0:T(128)S(1)} %copy-done.32, f32[32]{0:T(128)S(1)} %get-tuple-element.13), channel_id=1, replica_groups=mesh['gx'=2,'gy'=4,'gz'=4] {'gx','gy','gz'}, use_global_device_ids=true, to_apply=%region_7.8 | all-reduce | flops 128 | bytes 1024 | tf_op jit(solution)/shard_map/psum | solution.py:79
  137.4 4.1 %multiply_subtract_fusion = f32[32,6,10,130]{3,1,2,0:T(8,128)} fusion(f32[32,6,10,130]{3,1,2,0:T(8,128)} %copy-done.1, f32[32,8,12,132]{3,1,2,0:T(8,128)S(1)} %pad_maximum_fusion, f32[32]{0:T(128)S(1)} %mul.415, f32[32]{0:T(128)S(1)} %get-tuple-element.31), kind=kLoop, calls=%fused_computation.37 | loop fusion | flops 748800 | bytes 2995456 | tf_op jit(solution)/shard_map/sub | solution.py:100
  141.5 4.8 %copy.122 = f32[32,6,10,130]{0,3,2,1:T(8,128)} copy(f32[32,6,10,130]{3,1,2,0:T(8,128)} %multiply_subtract_fusion) | data formatting | bytes 1996800 | tf_op jit(solution)/shard_map/reshape | solution.py:111
  146.3 4.8 %reshape.172 = f32[32,7800]{0,1:T(8,128)} reshape(f32[32,6,10,130]{0,3,2,1:T(8,128)} %copy.122) | data formatting | bytes 1996800 | tf_op jit(solution)/shard_map/reshape | solution.py:111
  151.1 3.0 %gather_fusion.7 = f32[256,32]{1,0:T(8,128)S(1)} fusion(f32[32,7800]{0,1:T(8,128)} %reshape.172, s32[1024]{0:T(1024)} %get-tuple-element.84), kind=kCustom, calls=%fused_computation.5.clone | custom fusion | bytes 66560 | tf_op jit(solution)/shard_map/jit(_take)/gather | solution.py:116
  154.1 3.0 %gather_fusion.6 = f32[256,32]{1,0:T(8,128)S(1)} fusion(f32[32,7800]{0,1:T(8,128)} %reshape.172, s32[1024]{0:T(1024)} %get-tuple-element.85), kind=kCustom, calls=%fused_computation.4.clone | custom fusion | bytes 66560 | tf_op jit(solution)/shard_map/jit(_take)/gather | solution.py:115
  157.1 3.0 %gather_fusion.5 = f32[256,32]{1,0:T(8,128)S(1)} fusion(f32[32,7800]{0,1:T(8,128)} %reshape.172, s32[1024]{0:T(1024)} %get-tuple-element.86), kind=kCustom, calls=%fused_computation.3.clone | custom fusion | bytes 66560 | tf_op jit(solution)/shard_map/jit(_take)/gather | solution.py:116
  160.1 3.0 %gather_fusion.4 = f32[256,32]{1,0:T(8,128)S(1)} fusion(f32[32,7800]{0,1:T(8,128)} %reshape.172, s32[1024]{0:T(1024)} %get-tuple-element.87), kind=kCustom, calls=%fused_computation.2.clone | custom fusion | bytes 66560 | tf_op jit(solution)/shard_map/jit(_take)/gather | solution.py:115
  163.1 3.0 %gather_fusion.3 = f32[256,32]{1,0:T(8,128)S(1)} fusion(f32[32,7800]{0,1:T(8,128)} %reshape.172, s32[1024]{0:T(1024)} %get-tuple-element.88), kind=kCustom, calls=%fused_computation.1.clone | custom fusion | bytes 66560 | tf_op jit(solution)/shard_map/jit(_take)/gather | solution.py:116
  166.1 3.0 %gather_fusion.2 = f32[256,32]{1,0:T(8,128)S(1)} fusion(f32[32,7800]{0,1:T(8,128)} %reshape.172, s32[1024]{0:T(1024)} %get-tuple-element.89), kind=kCustom, calls=%fused_computation.clone | custom fusion | bytes 66560 | tf_op jit(solution)/shard_map/jit(_take)/gather | solution.py:115
  170.8 4.5 %all-to-all-start = ((f32[8,1,3072]{2,1,0:T(1,128)}), f32[8,1,3072]{2,1,0:T(1,128)S(1)}, u32[]{:S(2)}, u32[]{:S(2)}) async-start(f32[8,1,3072]{2,1,0:T(1,128)} %reshape.176), calls=%async_computation | async-start | bytes 196608 | tf_op jit(solution)/shard_map/all_to_all | solution.py:120
  175.3 7.2 %all-to-all-done = f32[8,1,3072]{2,1,0:T(1,128)S(1)} async-done(((f32[8,1,3072]{2,1,0:T(1,128)}), f32[8,1,3072]{2,1,0:T(1,128)S(1)}, u32[]{:S(2)}, u32[]{:S(2)}) %all-to-all-start) | async-done | bytes 98336 | tf_op jit(solution)/shard_map/all_to_all | solution.py:120
  (151 shorter events, 52.5 us)
Async XLA Ops:
  0.6 186.3 %copy-start = (f32[32,128]{1,0:T(8,128)S(1)}, f32[32,128]{1,0:T(8,128)}, u32[]{:S(2)}) copy-start(f32[32,128]{1,0:T(8,128)} %param.13) | copy-start | bytes 49156
  1.4 21.6 %collective-permute-start.6 = (s32[2,8,128]{2,1,0:T(8,128)S(1)}, s32[2,8,128]{2,1,0:T(8,128)S(1)}, u32[]{:S(2)}, u32[]{:S(2)}) collective-permute-start(s32[2,8,128]{2,1,0:T(8,128)S(1)} %get-tuple-element.58), channel_id=1, source_target_pairs={{0,16},{1,17},{2,18},{3,19},{4,20},{5,21},{6,22},{7,23},{8,24},{9,... | collective-permute-start | bytes 24584 | tf_op jit(solution)/shard_map/ppermute | solution.py:14
  6.3 16.7 %collective-permute-start.7 = (s32[2,8,128]{2,1,0:T(8,128)S(1)}, s32[2,8,128]{2,1,0:T(8,128)S(1)}, u32[]{:S(2)}, u32[]{:S(2)}) collective-permute-start(s32[2,8,128]{2,1,0:T(8,128)S(1)} %get-tuple-element.59), channel_id=1, source_target_pairs={{16,0},{17,1},{18,2},{19,3},{20,4},{21,5},{22,6},{23,7},{24,8},{25... | collective-permute-start | bytes 24584 | tf_op jit(solution)/shard_map/ppermute | solution.py:17
  8.7 34.5 %collective-permute-start = (f32[32,2,8,128]{3,2,1,0:T(8,128)S(1)}, f32[32,2,8,128]{3,2,1,0:T(8,128)S(1)}, u32[]{:S(2)}, u32[]{:S(2)}) collective-permute-start(f32[32,2,8,128]{3,2,1,0:T(8,128)S(1)} %get-tuple-element.39), channel_id=1, source_target_pairs={{0,16},{1,17},{2,18},{3,19},{4,20},{5,21},{6,22},{7,23},{8,24},{9,... | collective-permute-start | bytes 786440 | tf_op jit(solution)/shard_map/ppermute | solution.py:14
  13.2 30.1 %collective-permute-start.1 = (f32[32,2,8,128]{3,2,1,0:T(8,128)S(1)}, f32[32,2,8,128]{3,2,1,0:T(8,128)S(1)}, u32[]{:S(2)}, u32[]{:S(2)}) collective-permute-start(f32[32,2,8,128]{3,2,1,0:T(8,128)S(1)} %get-tuple-element.40), channel_id=1, source_target_pairs={{16,0},{17,1},{18,2},{19,3},{20,4},{21,5},{22,6},{23,7},{24,8},{25... | collective-permute-start | bytes 786440 | tf_op jit(solution)/shard_map/ppermute | solution.py:17
  23.0 5.4 %collective-permute-start.8 = (s32[8,2,128]{2,1,0:T(2,128)S(1)}, s32[8,2,128]{2,1,0:T(2,128)S(1)}, u32[]{:S(2)}, u32[]{:S(2)}) collective-permute-start(s32[8,2,128]{2,1,0:T(2,128)S(1)} %get-tuple-element.56), channel_id=1, source_target_pairs={{0,4},{4,8},{8,12},{1,5},{5,9},{9,13},{2,6},{6,10},{10,14},{3,7},{... | collective-permute-start | bytes 24584 | tf_op jit(solution)/shard_map/ppermute | solution.py:14
  26.4 5.5 %collective-permute-start.9 = (s32[8,2,128]{2,1,0:T(2,128)S(1)}, s32[8,2,128]{2,1,0:T(2,128)S(1)}, u32[]{:S(2)}, u32[]{:S(2)}) collective-permute-start(s32[8,2,128]{2,1,0:T(2,128)S(1)} %get-tuple-element.57), channel_id=1, source_target_pairs={{4,0},{8,4},{12,8},{5,1},{9,5},{13,9},{6,2},{10,6},{14,10},{7,3},{... | collective-permute-start | bytes 24584 | tf_op jit(solution)/shard_map/ppermute | solution.py:17
  32.1 3.8 %collective-permute-start.10 = (s32[8,12,2]{2,1,0:T(8,128)S(1)}, s32[8,12,2]{2,1,0:T(8,128)S(1)}, u32[]{:S(2)}, u32[]{:S(2)}) collective-permute-start(s32[8,12,2]{2,1,0:T(8,128)S(1)} %get-tuple-element.54), channel_id=1, source_target_pairs={{0,1},{1,2},{2,3},{4,5},{5,6},{6,7},{8,9},{9,10},{10,11},{12,13},{... | collective-permute-start | bytes 2312 | tf_op jit(solution)/shard_map/ppermute | solution.py:14
  33.4 4.9 %collective-permute-start.11 = (s32[8,12,2]{2,1,0:T(8,128)S(1)}, s32[8,12,2]{2,1,0:T(8,128)S(1)}, u32[]{:S(2)}, u32[]{:S(2)}) collective-permute-start(s32[8,12,2]{2,1,0:T(8,128)S(1)} %get-tuple-element.55), channel_id=1, source_target_pairs={{1,0},{2,1},{3,2},{5,4},{6,5},{7,6},{9,8},{10,9},{11,10},{13,12},{... | collective-permute-start | bytes 2312 | tf_op jit(solution)/shard_map/ppermute | solution.py:17
  35.9 20.7 %copy-start.4 = (f32[32,4,8,128]{3,1,2,0:T(4,128)}, f32[32,4,8,128]{3,1,2,0:T(4,128)S(1)}, u32[]{:S(2)}) copy-start(f32[32,4,8,128]{3,1,2,0:T(4,128)S(1)} %copy.105) | copy-start | bytes 1572868
  43.5 14.2 %copy-start.7 = (f32[32,2,8,128]{3,1,2,0:T(2,128)}, f32[32,2,8,128]{3,1,2,0:T(2,128)S(1)}, u32[]{:S(2)}) copy-start(f32[32,2,8,128]{3,1,2,0:T(2,128)S(1)} %copy.92) | copy-start | bytes 786436
  43.7 8.2 %collective-permute-start.2 = (f32[32,8,2,128]{3,1,2,0:T(8,128)S(1)}, f32[32,8,2,128]{3,1,2,0:T(8,128)S(1)}, u32[]{:S(2)}, u32[]{:S(2)}) collective-permute-start(f32[32,8,2,128]{3,1,2,0:T(8,128)S(1)} %get-tuple-element.37), channel_id=1, source_target_pairs={{0,4},{4,8},{8,12},{1,5},{5,9},{9,13},{2,6},{6,10},{10,14},{3,7},{... | collective-permute-start | bytes 786440 | tf_op jit(solution)/shard_map/ppermute | solution.py:14
  47.2 9.4 %collective-permute-start.3 = (f32[32,8,2,128]{3,1,2,0:T(8,128)S(1)}, f32[32,8,2,128]{3,1,2,0:T(8,128)S(1)}, u32[]{:S(2)}, u32[]{:S(2)}) collective-permute-start(f32[32,8,2,128]{3,1,2,0:T(8,128)S(1)} %get-tuple-element.38), channel_id=1, source_target_pairs={{4,0},{8,4},{12,8},{5,1},{9,5},{13,9},{6,2},{10,6},{14,10},{7,3},{... | collective-permute-start | bytes 786440 | tf_op jit(solution)/shard_map/ppermute | solution.py:17
  62.5 14.3 %collective-permute-start.5 = (f32[32,8,12,2]{0,1,3,2:T(8,128)S(1)}, f32[32,8,12,2]{0,1,3,2:T(8,128)S(1)}, u32[]{:S(2)}, u32[]{:S(2)}) collective-permute-start(f32[32,8,12,2]{0,1,3,2:T(8,128)S(1)} %copy.94), channel_id=1, source_target_pairs={{1,0},{2,1},{3,2},{5,4},{6,5},{7,6},{9,8},{10,9},{11,10},{13,12},{... | collective-permute-start | bytes 73736 | tf_op jit(solution)/shard_map/ppermute | solution.py:17
  63.8 10.7 %collective-permute-start.4 = (f32[32,8,12,2]{0,1,3,2:T(8,128)S(1)}, f32[32,8,12,2]{0,1,3,2:T(8,128)S(1)}, u32[]{:S(2)}, u32[]{:S(2)}) collective-permute-start(f32[32,8,12,2]{0,1,3,2:T(8,128)S(1)} %copy.93), channel_id=1, source_target_pairs={{0,1},{1,2},{2,3},{4,5},{5,6},{6,7},{8,9},{9,10},{10,11},{12,13},{... | collective-permute-start | bytes 73736 | tf_op jit(solution)/shard_map/ppermute | solution.py:14
  146.3 22.8 %copy-start.26 = (f32[256]{0:T(256)S(1)}, f32[256]{0:T(256)}, u32[]{:S(2)}) copy-start(f32[256]{0:T(256)} %select_multiply_fusion) | copy-start | bytes 3076
  146.3 22.8 %copy-start.27 = (pred[256]{0:T(512)(128)(4,1)S(1)}, pred[256]{0:T(512)(128)(4,1)}, u32[]{:S(2)}) copy-start(pred[256]{0:T(512)(128)(4,1)} %get-tuple-element.63) | copy-start | bytes 772
  146.3 22.8 %copy-start.28 = (pred[256]{0:T(512)(128)(4,1)S(1)}, pred[256]{0:T(512)(128)(4,1)}, u32[]{:S(2)}) copy-start(pred[256]{0:T(512)(128)(4,1)} %get-tuple-element.64) | copy-start | bytes 772
  146.3 22.8 %copy-start.29 = (pred[256]{0:T(512)(128)(4,1)S(1)}, pred[256]{0:T(512)(128)(4,1)}, u32[]{:S(2)}) copy-start(pred[256]{0:T(512)(128)(4,1)} %get-tuple-element.65) | copy-start | bytes 772
  146.3 22.8 %copy-start.30 = (pred[256]{0:T(512)(128)(4,1)S(1)}, pred[256]{0:T(512)(128)(4,1)}, u32[]{:S(2)}) copy-start(pred[256]{0:T(512)(128)(4,1)} %get-tuple-element.66) | copy-start | bytes 772
  146.3 22.8 %copy-start.31 = (pred[256]{0:T(512)(128)(4,1)S(1)}, pred[256]{0:T(512)(128)(4,1)}, u32[]{:S(2)}) copy-start(pred[256]{0:T(512)(128)(4,1)} %get-tuple-element.67) | copy-start | bytes 772
  146.3 22.8 %copy-start.33 = (pred[256]{0:T(512)(128)(4,1)S(1)}, pred[256]{0:T(512)(128)(4,1)}, u32[]{:S(2)}) copy-start(pred[256]{0:T(512)(128)(4,1)} %get-tuple-element.29) | copy-start | bytes 772
  154.1 21.2 %copy-start.34 = (s32[128]{0:T(128)S(1)}, s32[128]{0:T(128)}, u32[]{:S(2)}) copy-start(s32[128]{0:T(128)} %param.12) | copy-start | bytes 1540
  170.8 11.8 %all-to-all-start = ((f32[8,1,3072]{2,1,0:T(1,128)}), f32[8,1,3072]{2,1,0:T(1,128)S(1)}, u32[]{:S(2)}, u32[]{:S(2)}) async-start(f32[8,1,3072]{2,1,0:T(1,128)} %reshape.176), calls=%async_computation | async-start | bytes 196608 | tf_op jit(solution)/shard_map/all_to_all | solution.py:120
  (24 other events, 145.9 us)
where the time goes:
time: 190 us; the launch traced here: 189 us
  local copies, waits for them, and re-layouts  55.5 us (29%)
  blocking collectives  41.9 us (22%)
  other arithmetic  36.8 us (19%)
  starting transfers between devices  34.2 us (18%)
  waiting for transfers between devices  18.6 us (10%)
    psum x1, blocking collectives, per_device(): lax.psum((local_inner(source_term, source_term), local_inner(source_term,...  41.9 us
    ppermute x6, starting transfers between devices, extended(): lax.ppermute(lax.slice_in_dim(block, block.shape[dim] - width, None, axis...  21.9 us
    ppermute x6, waiting for transfers between devices, extended(): lax.ppermute(lax.slice_in_dim(block, 0, width, axis=dim), axis, backward)  10.7 us
    reshape x2, local copies, waits for them, and re-layouts, per_device(): flattened = solution_pad.reshape(sensors, -1)  9.57 us
    gather x3, local copies, waits for them, and re-layouts, gradient(): upper = jnp.take(flattened, centre + stride, axis=1)  8.98 us
    gather x3, local copies, waits for them, and re-layouts, gradient(): lower = jnp.take(flattened, centre - stride, axis=1)  8.97 us
    ppermute x6, starting transfers between devices, extended(): lax.ppermute(lax.slice_in_dim(block, 0, width, axis=dim), axis, backward)  7.75 us
    all_to_all x1, waiting for transfers between devices, per_device(): lax.all_to_all(columns, ('gx', 'gy'), split_axis=2, concat_axis=2, tiled=...  7.24 us
  transfers between devices with their start and end apart: 13, of which 5 were waited for; matrix products, arithmetic and copies ran while one was open for 15% of the time, Pallas kernels for 0%

commit v1 on v0

--- a/solution.py
+++ b/solution.py
@@ -77,13 +77,16 @@
     twice_applied = stencil(applied, inner_cond, inner_in)
     applied_core = applied[:, 1:-1, 1:-1, 1:-1]
     moment_zero, moment_one, moment_two, moment_three = lax.psum(
-        (
-            local_inner(source_term, source_term),
-            local_inner(source_term, applied_core),
-            local_inner(applied_core, applied_core),
-            local_inner(applied_core, twice_applied),
+        lax.psum(
+            (
+                local_inner(source_term, source_term),
+                local_inner(source_term, applied_core),
+                local_inner(applied_core, applied_core),
+                local_inner(applied_core, twice_applied),
+            ),
+            ("gy", "gz"),
         ),
-        ("gx", "gy", "gz"),
+        "gx",
     )
     first_step = moment_zero / moment_one
     residue = first_step * first_step * moment_two - moment_zero

time: 190 us -> 184 us (0.968)
  blocking collectives: 41.9 us -> 37 us
    psum x1, blocking collectives: 41.9 us -> 31.2 us  [per_device(): lax.psum((local_inner(source_term, source_term), local_inner(source_term,...]
    psum x0 -> x1, blocking collectives: none -> 5.76 us  [per_device(): lax.psum(lax.psum((local_inner(source_term, source_term), local_inner(sou...]
where the time goes in v1:
time: 184 us; the launch traced here: 183 us
  local copies, waits for them, and re-layouts  55.5 us (30%)
  other arithmetic  37 us (20%)
  blocking collectives  37 us (20%)
  starting transfers between devices  33 us (18%)
  waiting for transfers between devices  18.6 us (10%)
    psum x1, blocking collectives, per_device(): lax.psum((local_inner(source_term, source_term), local_inner(source_term,...  31.2 us
    ppermute x6, starting transfers between devices, extended(): lax.ppermute(lax.slice_in_dim(block, block.shape[dim] - width, None, axis...  21.9 us
    ppermute x6, waiting for transfers between devices, extended(): lax.ppermute(lax.slice_in_dim(block, 0, width, axis=dim), axis, backward)  10.7 us
    reshape x2, local copies, waits for them, and re-layouts, per_device(): flattened = solution_pad.reshape(sensors, -1)  9.56 us
    gather x3, local copies, waits for them, and re-layouts, gradient(): upper = jnp.take(flattened, centre + stride, axis=1)  8.98 us
    gather x3, local copies, waits for them, and re-layouts, gradient(): lower = jnp.take(flattened, centre - stride, axis=1)  8.97 us
    ppermute x6, starting transfers between devices, extended(): lax.ppermute(lax.slice_in_dim(block, 0, width, axis=dim), axis, backward)  7.75 us
    add x1, other arithmetic, stencil(): accumulated = accumulated + weight * (centre - padded[leading + beside_all])  7.22 us
  transfers between devices with their start and end apart: 13, of which 5 were waited for; matrix products, arithmetic and copies ran while one was open for 15% of the time, Pallas kernels for 0%

profile of v1, /device:TPU:0, one launch (start us, length us, event | category | flops | bytes accessed | tf_op | source)
XLA Modules:
  0.0 182.8 jit_solution(5269733238857885998)
XLA Ops:
  1.4 4.9 %collective-permute-start.6 = (s32[2,8,128]{2,1,0:T(8,128)S(1)}, s32[2,8,128]{2,1,0:T(8,128)S(1)}, u32[]{:S(2)}, u32[]{:S(2)}) collective-permute-start(s32[2,8,128]{2,1,0:T(8,128)S(1)} %get-tuple-element.62), channel_id=1, source_target_pairs={{0,16},{1,17},{2,18},{3,19},{4,20},{5,21},{6,22},{7,23},{8,24},{9,... | collective-permute-start | bytes 24584 | tf_op jit(solution)/shard_map/ppermute | solution.py:14
  8.7 4.6 %collective-permute-start = (f32[32,2,8,128]{3,2,1,0:T(8,128)S(1)}, f32[32,2,8,128]{3,2,1,0:T(8,128)S(1)}, u32[]{:S(2)}, u32[]{:S(2)}) collective-permute-start(f32[32,2,8,128]{3,2,1,0:T(8,128)S(1)} %get-tuple-element.43), channel_id=1, source_target_pairs={{0,16},{1,17},{2,18},{3,19},{4,20},{5,21},{6,22},{7,23},{8,24},{9,... | collective-permute-start | bytes 786440 | tf_op jit(solution)/shard_map/ppermute | solution.py:14
  23.1 3.5 %collective-permute-start.8 = (s32[8,2,128]{2,1,0:T(2,128)S(1)}, s32[8,2,128]{2,1,0:T(2,128)S(1)}, u32[]{:S(2)}, u32[]{:S(2)}) collective-permute-start(s32[8,2,128]{2,1,0:T(2,128)S(1)} %get-tuple-element.60), channel_id=1, source_target_pairs={{0,4},{4,8},{8,12},{1,5},{5,9},{9,13},{2,6},{6,10},{10,14},{3,7},{... | collective-permute-start | bytes 24584 | tf_op jit(solution)/shard_map/ppermute | solution.py:14
  28.4 3.6 %collective-permute-done.9 = s32[8,2,128]{2,1,0:T(2,128)S(1)} collective-permute-done((s32[8,2,128]{2,1,0:T(2,128)S(1)}, s32[8,2,128]{2,1,0:T(2,128)S(1)}, u32[]{:S(2)}, u32[]{:S(2)}) %collective-permute-start.9) | collective-permute-done | bytes 8224 | tf_op jit(solution)/shard_map/ppermute | solution.py:17
  38.5 3.9 %select_add_fusion = f32[8,12,132]{2,1,0:T(8,128)S(1)} fusion(f32[]{:T(128)} %bitcast.8, f32[]{:T(128)} %bitcast.7, f32[]{:T(128)} %bitcast.6, f32[]{:T(128)} %bitcast.5, f32[]{:T(128)} %bitcast.4, f32[]{:T(128)} %bitcast.3, s32[8,12,2]{2,1,0:T(8,128)S(1)} %collective-permute-done.11, s32[8,2,128]{2,1,0:T(2,128)S(1)} %collective-permute-done.9, ...), kind=kLoop, calls=%fused_computation.79 | loop fusion | flops 291456 | bytes 101400 | tf_op jit(solution)/shard_map/add | solution.py:25
  43.9 3.5 %collective-permute-start.2 = (f32[32,8,2,128]{3,1,2,0:T(8,128)S(1)}, f32[32,8,2,128]{3,1,2,0:T(8,128)S(1)}, u32[]{:S(2)}, u32[]{:S(2)}) collective-permute-start(f32[32,8,2,128]{3,1,2,0:T(8,128)S(1)} %get-tuple-element.41), channel_id=1, source_target_pairs={{0,4},{4,8},{8,12},{1,5},{5,9},{9,13},{2,6},{6,10},{10,14},{3,7},{... | collective-permute-start | bytes 786440 | tf_op jit(solution)/shard_map/ppermute | solution.py:14
  52.1 4.7 %collective-permute-done.3 = f32[32,8,2,128]{3,1,2,0:T(8,128)S(1)} collective-permute-done((f32[32,8,2,128]{3,1,2,0:T(8,128)S(1)}, f32[32,8,2,128]{3,1,2,0:T(8,128)S(1)}, u32[]{:S(2)}, u32[]{:S(2)}) %collective-permute-start.3) | collective-permute-done | bytes 262176 | tf_op jit(solution)/shard_map/ppermute | solution.py:17
  64.0 4.2 %collective-permute-start.4 = (f32[32,8,12,2]{0,1,3,2:T(8,128)S(1)}, f32[32,8,12,2]{0,1,3,2:T(8,128)S(1)}, u32[]{:S(2)}, u32[]{:S(2)}) collective-permute-start(f32[32,8,12,2]{0,1,3,2:T(8,128)S(1)} %copy.93), channel_id=1, source_target_pairs={{0,1},{1,2},{2,3},{4,5},{5,6},{6,7},{8,9},{9,10},{10,11},{12,13},{... | collective-permute-start | bytes 73736 | tf_op jit(solution)/shard_map/ppermute | solution.py:14
  77.1 2.4 %copy.96 = f32[32,8,12,2]{3,1,2,0:T(8,128)} copy(f32[32,8,12,2]{0,1,3,2:T(8,128)S(1)} %collective-permute-done.5) | data formatting | bytes 49152 | tf_op jit(solution)/shard_map/ppermute | solution.py:17
  79.6 4.8 %pad_maximum_fusion = f32[32,8,12,132]{3,1,2,0:T(8,128)S(1)} fusion(f32[32,8,12,2]{3,1,2,0:T(8,128)} %copy.96, f32[32,8,2,128]{3,1,2,0:T(8,128)} %copy-done.11, f32[32,2,8,128]{3,1,2,0:T(2,128)} %copy-done.7, f32[32,4,8,128]{3,1,2,0:T(4,128)} %copy-done.4, f32[32,2,8,128]{3,1,2,0:T(2,128)S(1)} %copy.90, f32[32,8,2,128]{3,1,2,0:T(8,128)} %copy-done.9, ...), kind=kLoop, calls=%fused_computation.8 | loop fusion | flops 2433024 | bytes 3244032 | tf_op jit(solution)/shard_map/concatenate | solution.py:18
  84.5 7.2 %fusion.2 = f32[32,6,10,130]{3,1,2,0:T(8,128)S(1)} fusion(f32[32,8,12,2]{3,1,2,0:T(8,128)S(1)} %copy-done.3, f32[32,8,2,128]{3,1,2,0:T(8,128)S(1)} %copy-done.12, f32[32,8,2,128]{3,1,2,0:T(8,128)S(1)} %copy-done.10, f32[32,2,8,128]{3,1,2,0:T(2,128)S(1)} %copy-done.8, f32[32,4,8,128]{3,1,2,0:T(4,128)S(1)} %copy-done.5, f32[32,2,8,128]{3,1,2,0:T(2,128)S(1)} %copy.90, ...), kind=kLoop, calls=%fused_computation.12 | loop fusion | flops 7238400 | bytes 7799616 | tf_op jit(solution)/shard_map/add | solution.py:49
  95.7 31.2 %all-reduce = (f32[32]{0:T(128)S(1)}, f32[32]{0:T(128)S(1)}, f32[32]{0:T(128)S(1)}, f32[32]{0:T(128)S(1)}) all-reduce(f32[32]{0:T(128)S(1)} %get-tuple-element.15, f32[32]{0:T(128)S(1)} %get-tuple-element.14, f32[32]{0:T(128)S(1)} %copy-done.32, f32[32]{0:T(128)S(1)} %get-tuple-element.13), channel_id=1, replica_groups=mesh['gx'=2,'gy'=4,'gz'=4] {'gy','gz'}, use_global_device_ids=true, to_apply=%region_10.11 | all-reduce | flops 128 | bytes 1024 | tf_op jit(solution)/shard_map/psum | solution.py:80
  126.9 5.8 %all-reduce.1 = (f32[32]{0:T(128)S(1)}, f32[32]{0:T(128)S(1)}, f32[32]{0:T(128)S(1)}, f32[32]{0:T(128)S(1)}) all-reduce(f32[32]{0:T(128)S(1)} %get-tuple-element.25, f32[32]{0:T(128)S(1)} %get-tuple-element.26, f32[32]{0:T(128)S(1)} %get-tuple-element.27, f32[32]{0:T(128)S(1)} %get-tuple-element.28), channel_id=1, replica_groups=mesh['gx'=2,'gy'=4,'gz'=4] {'gx'}, use_global_device_ids=true, to_apply=%region_11.12 | all-reduce | flops 128 | bytes 1024 | tf_op jit(solution)/shard_map/psum | solution.py:79
  132.7 4.1 %multiply_subtract_fusion = f32[32,6,10,130]{3,1,2,0:T(8,128)} fusion(f32[32,6,10,130]{3,1,2,0:T(8,128)} %copy-done.1, f32[32,8,12,132]{3,1,2,0:T(8,128)S(1)} %pad_maximum_fusion, f32[32]{0:T(128)S(1)} %mul.415, f32[32]{0:T(128)S(1)} %get-tuple-element.35), kind=kLoop, calls=%fused_computation.37 | loop fusion | flops 748800 | bytes 2995456 | tf_op jit(solution)/shard_map/sub | solution.py:103
  136.8 4.8 %copy.122 = f32[32,6,10,130]{0,3,2,1:T(8,128)} copy(f32[32,6,10,130]{3,1,2,0:T(8,128)} %multiply_subtract_fusion) | data formatting | bytes 1996800 | tf_op jit(solution)/shard_map/reshape | solution.py:114
  141.6 4.8 %reshape.172 = f32[32,7800]{0,1:T(8,128)} reshape(f32[32,6,10,130]{0,3,2,1:T(8,128)} %copy.122) | data formatting | bytes 1996800 | tf_op jit(solution)/shard_map/reshape | solution.py:114
  146.4 3.0 %gather_fusion.7 = f32[256,32]{1,0:T(8,128)S(1)} fusion(f32[32,7800]{0,1:T(8,128)} %reshape.172, s32[1024]{0:T(1024)} %get-tuple-element.88), kind=kCustom, calls=%fused_computation.5.clone | custom fusion | bytes 66560 | tf_op jit(solution)/shard_map/jit(_take)/gather | solution.py:119
  149.4 3.0 %gather_fusion.6 = f32[256,32]{1,0:T(8,128)S(1)} fusion(f32[32,7800]{0,1:T(8,128)} %reshape.172, s32[1024]{0:T(1024)} %get-tuple-element.89), kind=kCustom, calls=%fused_computation.4.clone | custom fusion | bytes 66560 | tf_op jit(solution)/shard_map/jit(_take)/gather | solution.py:118
  152.4 3.0 %gather_fusion.5 = f32[256,32]{1,0:T(8,128)S(1)} fusion(f32[32,7800]{0,1:T(8,128)} %reshape.172, s32[1024]{0:T(1024)} %get-tuple-element.90), kind=kCustom, calls=%fused_computation.3.clone | custom fusion | bytes 66560 | tf_op jit(solution)/shard_map/jit(_take)/gather | solution.py:119
  155.4 3.0 %gather_fusion.4 = f32[256,32]{1,0:T(8,128)S(1)} fusion(f32[32,7800]{0,1:T(8,128)} %reshape.172, s32[1024]{0:T(1024)} %get-tuple-element.91), kind=kCustom, calls=%fused_computation.2.clone | custom fusion | bytes 66560 | tf_op jit(solution)/shard_map/jit(_take)/gather | solution.py:118
  158.4 3.0 %gather_fusion.3 = f32[256,32]{1,0:T(8,128)S(1)} fusion(f32[32,7800]{0,1:T(8,128)} %reshape.172, s32[1024]{0:T(1024)} %get-tuple-element.92), kind=kCustom, calls=%fused_computation.1.clone | custom fusion | bytes 66560 | tf_op jit(solution)/shard_map/jit(_take)/gather | solution.py:119
  161.4 3.0 %gather_fusion.2 = f32[256,32]{1,0:T(8,128)S(1)} fusion(f32[32,7800]{0,1:T(8,128)} %reshape.172, s32[1024]{0:T(1024)} %get-tuple-element.93), kind=kCustom, calls=%fused_computation.clone | custom fusion | bytes 66560 | tf_op jit(solution)/shard_map/jit(_take)/gather | solution.py:118
  166.1 3.4 %all-to-all-start = ((f32[8,1,3072]{2,1,0:T(1,128)}), f32[8,1,3072]{2,1,0:T(1,128)S(1)}, u32[]{:S(2)}, u32[]{:S(2)}) async-start(f32[8,1,3072]{2,1,0:T(1,128)} %reshape.176), calls=%async_computation | async-start | bytes 196608 | tf_op jit(solution)/shard_map/all_to_all | solution.py:123
  169.4 7.2 %all-to-all-done = f32[8,1,3072]{2,1,0:T(1,128)S(1)} async-done(((f32[8,1,3072]{2,1,0:T(1,128)}), f32[8,1,3072]{2,1,0:T(1,128)S(1)}, u32[]{:S(2)}, u32[]{:S(2)}) %all-to-all-start) | async-done | bytes 98336 | tf_op jit(solution)/shard_map/all_to_all | solution.py:123
  (152 shorter events, 54.9 us)
Async XLA Ops:
  0.6 180.4 %copy-start = (f32[32,128]{1,0:T(8,128)S(1)}, f32[32,128]{1,0:T(8,128)}, u32[]{:S(2)}) copy-start(f32[32,128]{1,0:T(8,128)} %param.13) | copy-start | bytes 49156
  1.4 21.7 %collective-permute-start.6 = (s32[2,8,128]{2,1,0:T(8,128)S(1)}, s32[2,8,128]{2,1,0:T(8,128)S(1)}, u32[]{:S(2)}, u32[]{:S(2)}) collective-permute-start(s32[2,8,128]{2,1,0:T(8,128)S(1)} %get-tuple-element.62), channel_id=1, source_target_pairs={{0,16},{1,17},{2,18},{3,19},{4,20},{5,21},{6,22},{7,23},{8,24},{9,... | collective-permute-start | bytes 24584 | tf_op jit(solution)/shard_map/ppermute | solution.py:14
  6.3 16.8 %collective-permute-start.7 = (s32[2,8,128]{2,1,0:T(8,128)S(1)}, s32[2,8,128]{2,1,0:T(8,128)S(1)}, u32[]{:S(2)}, u32[]{:S(2)}) collective-permute-start(s32[2,8,128]{2,1,0:T(8,128)S(1)} %get-tuple-element.63), channel_id=1, source_target_pairs={{16,0},{17,1},{18,2},{19,3},{20,4},{21,5},{22,6},{23,7},{24,8},{25... | collective-permute-start | bytes 24584 | tf_op jit(solution)/shard_map/ppermute | solution.py:17
  8.7 34.8 %collective-permute-start = (f32[32,2,8,128]{3,2,1,0:T(8,128)S(1)}, f32[32,2,8,128]{3,2,1,0:T(8,128)S(1)}, u32[]{:S(2)}, u32[]{:S(2)}) collective-permute-start(f32[32,2,8,128]{3,2,1,0:T(8,128)S(1)} %get-tuple-element.43), channel_id=1, source_target_pairs={{0,16},{1,17},{2,18},{3,19},{4,20},{5,21},{6,22},{7,23},{8,24},{9,... | collective-permute-start | bytes 786440 | tf_op jit(solution)/shard_map/ppermute | solution.py:14
  13.2 30.4 %collective-permute-start.1 = (f32[32,2,8,128]{3,2,1,0:T(8,128)S(1)}, f32[32,2,8,128]{3,2,1,0:T(8,128)S(1)}, u32[]{:S(2)}, u32[]{:S(2)}) collective-permute-start(f32[32,2,8,128]{3,2,1,0:T(8,128)S(1)} %get-tuple-element.44), channel_id=1, source_target_pairs={{16,0},{17,1},{18,2},{19,3},{20,4},{21,5},{22,6},{23,7},{24,8},{25... | collective-permute-start | bytes 786440 | tf_op jit(solution)/shard_map/ppermute | solution.py:17
  23.1 5.4 %collective-permute-start.8 = (s32[8,2,128]{2,1,0:T(2,128)S(1)}, s32[8,2,128]{2,1,0:T(2,128)S(1)}, u32[]{:S(2)}, u32[]{:S(2)}) collective-permute-start(s32[8,2,128]{2,1,0:T(2,128)S(1)} %get-tuple-element.60), channel_id=1, source_target_pairs={{0,4},{4,8},{8,12},{1,5},{5,9},{9,13},{2,6},{6,10},{10,14},{3,7},{... | collective-permute-start | bytes 24584 | tf_op jit(solution)/shard_map/ppermute | solution.py:14
  26.5 5.5 %collective-permute-start.9 = (s32[8,2,128]{2,1,0:T(2,128)S(1)}, s32[8,2,128]{2,1,0:T(2,128)S(1)}, u32[]{:S(2)}, u32[]{:S(2)}) collective-permute-start(s32[8,2,128]{2,1,0:T(2,128)S(1)} %get-tuple-element.61), channel_id=1, source_target_pairs={{4,0},{8,4},{12,8},{5,1},{9,5},{13,9},{6,2},{10,6},{14,10},{7,3},{... | collective-permute-start | bytes 24584 | tf_op jit(solution)/shard_map/ppermute | solution.py:17
  32.2 3.8 %collective-permute-start.10 = (s32[8,12,2]{2,1,0:T(8,128)S(1)}, s32[8,12,2]{2,1,0:T(8,128)S(1)}, u32[]{:S(2)}, u32[]{:S(2)}) collective-permute-start(s32[8,12,2]{2,1,0:T(8,128)S(1)} %get-tuple-element.58), channel_id=1, source_target_pairs={{0,1},{1,2},{2,3},{4,5},{5,6},{6,7},{8,9},{9,10},{10,11},{12,13},{... | collective-permute-start | bytes 2312 | tf_op jit(solution)/shard_map/ppermute | solution.py:14
  33.5 4.9 %collective-permute-start.11 = (s32[8,12,2]{2,1,0:T(8,128)S(1)}, s32[8,12,2]{2,1,0:T(8,128)S(1)}, u32[]{:S(2)}, u32[]{:S(2)}) collective-permute-start(s32[8,12,2]{2,1,0:T(8,128)S(1)} %get-tuple-element.59), channel_id=1, source_target_pairs={{1,0},{2,1},{3,2},{5,4},{6,5},{7,6},{9,8},{10,9},{11,10},{13,12},{... | collective-permute-start | bytes 2312 | tf_op jit(solution)/shard_map/ppermute | solution.py:17
  36.0 20.8 %copy-start.4 = (f32[32,4,8,128]{3,1,2,0:T(4,128)}, f32[32,4,8,128]{3,1,2,0:T(4,128)S(1)}, u32[]{:S(2)}) copy-start(f32[32,4,8,128]{3,1,2,0:T(4,128)S(1)} %copy.105) | copy-start | bytes 1572868
  43.7 14.2 %copy-start.7 = (f32[32,2,8,128]{3,1,2,0:T(2,128)}, f32[32,2,8,128]{3,1,2,0:T(2,128)S(1)}, u32[]{:S(2)}) copy-start(f32[32,2,8,128]{3,1,2,0:T(2,128)S(1)} %copy.92) | copy-start | bytes 786436
  43.9 8.2 %collective-permute-start.2 = (f32[32,8,2,128]{3,1,2,0:T(8,128)S(1)}, f32[32,8,2,128]{3,1,2,0:T(8,128)S(1)}, u32[]{:S(2)}, u32[]{:S(2)}) collective-permute-start(f32[32,8,2,128]{3,1,2,0:T(8,128)S(1)} %get-tuple-element.41), channel_id=1, source_target_pairs={{0,4},{4,8},{8,12},{1,5},{5,9},{9,13},{2,6},{6,10},{10,14},{3,7},{... | collective-permute-start | bytes 786440 | tf_op jit(solution)/shard_map/ppermute | solution.py:14
  47.4 9.4 %collective-permute-start.3 = (f32[32,8,2,128]{3,1,2,0:T(8,128)S(1)}, f32[32,8,2,128]{3,1,2,0:T(8,128)S(1)}, u32[]{:S(2)}, u32[]{:S(2)}) collective-permute-start(f32[32,8,2,128]{3,1,2,0:T(8,128)S(1)} %get-tuple-element.42), channel_id=1, source_target_pairs={{4,0},{8,4},{12,8},{5,1},{9,5},{13,9},{6,2},{10,6},{14,10},{7,3},{... | collective-permute-start | bytes 786440 | tf_op jit(solution)/shard_map/ppermute | solution.py:17
  62.7 14.3 %collective-permute-start.5 = (f32[32,8,12,2]{0,1,3,2:T(8,128)S(1)}, f32[32,8,12,2]{0,1,3,2:T(8,128)S(1)}, u32[]{:S(2)}, u32[]{:S(2)}) collective-permute-start(f32[32,8,12,2]{0,1,3,2:T(8,128)S(1)} %copy.94), channel_id=1, source_target_pairs={{1,0},{2,1},{3,2},{5,4},{6,5},{7,6},{9,8},{10,9},{11,10},{13,12},{... | collective-permute-start | bytes 73736 | tf_op jit(solution)/shard_map/ppermute | solution.py:17
  64.0 10.7 %collective-permute-start.4 = (f32[32,8,12,2]{0,1,3,2:T(8,128)S(1)}, f32[32,8,12,2]{0,1,3,2:T(8,128)S(1)}, u32[]{:S(2)}, u32[]{:S(2)}) collective-permute-start(f32[32,8,12,2]{0,1,3,2:T(8,128)S(1)} %copy.93), channel_id=1, source_target_pairs={{0,1},{1,2},{2,3},{4,5},{5,6},{6,7},{8,9},{9,10},{10,11},{12,13},{... | collective-permute-start | bytes 73736 | tf_op jit(solution)/shard_map/ppermute | solution.py:14
  141.6 22.8 %copy-start.26 = (f32[256]{0:T(256)S(1)}, f32[256]{0:T(256)}, u32[]{:S(2)}) copy-start(f32[256]{0:T(256)} %select_multiply_fusion) | copy-start | bytes 3076
  141.6 22.8 %copy-start.27 = (pred[256]{0:T(512)(128)(4,1)S(1)}, pred[256]{0:T(512)(128)(4,1)}, u32[]{:S(2)}) copy-start(pred[256]{0:T(512)(128)(4,1)} %get-tuple-element.67) | copy-start | bytes 772
  141.6 22.8 %copy-start.28 = (pred[256]{0:T(512)(128)(4,1)S(1)}, pred[256]{0:T(512)(128)(4,1)}, u32[]{:S(2)}) copy-start(pred[256]{0:T(512)(128)(4,1)} %get-tuple-element.68) | copy-start | bytes 772
  141.6 22.8 %copy-start.29 = (pred[256]{0:T(512)(128)(4,1)S(1)}, pred[256]{0:T(512)(128)(4,1)}, u32[]{:S(2)}) copy-start(pred[256]{0:T(512)(128)(4,1)} %get-tuple-element.69) | copy-start | bytes 772
  141.6 22.8 %copy-start.30 = (pred[256]{0:T(512)(128)(4,1)S(1)}, pred[256]{0:T(512)(128)(4,1)}, u32[]{:S(2)}) copy-start(pred[256]{0:T(512)(128)(4,1)} %get-tuple-element.70) | copy-start | bytes 772
  141.6 22.8 %copy-start.31 = (pred[256]{0:T(512)(128)(4,1)S(1)}, pred[256]{0:T(512)(128)(4,1)}, u32[]{:S(2)}) copy-start(pred[256]{0:T(512)(128)(4,1)} %get-tuple-element.71) | copy-start | bytes 772
  141.6 22.8 %copy-start.33 = (pred[256]{0:T(512)(128)(4,1)S(1)}, pred[256]{0:T(512)(128)(4,1)}, u32[]{:S(2)}) copy-start(pred[256]{0:T(512)(128)(4,1)} %get-tuple-element.33) | copy-start | bytes 772
  149.4 20.0 %copy-start.34 = (s32[128]{0:T(128)S(1)}, s32[128]{0:T(128)}, u32[]{:S(2)}) copy-start(s32[128]{0:T(128)} %param.12) | copy-start | bytes 1540
  166.1 10.6 %all-to-all-start = ((f32[8,1,3072]{2,1,0:T(1,128)}), f32[8,1,3072]{2,1,0:T(1,128)S(1)}, u32[]{:S(2)}, u32[]{:S(2)}) async-start(f32[8,1,3072]{2,1,0:T(1,128)} %reshape.176), calls=%async_computation | async-start | bytes 196608 | tf_op jit(solution)/shard_map/all_to_all | solution.py:123
  (24 other events, 145.8 us)
